TPU v7x, 32 devices: a whole 2x2x4 slice. The times are simulated.
32 devices in a mesh: wide: 8 (over y, x, core), blk: 4 (over z).
Axes of the slice: x: 2, y: 2, z: 4, core: 2. Of those that a mesh axis runs over, the one named last changes fastest.
Arguments:
- left_points: float32 [4096], P(('wide', 'blk')), may hold values from -1 to 1, as said below
- left_ports: int32 [4096], P(('wide', 'blk')), may hold values from 0 to 63
- left_values: bfloat16 [4096, 64], P(('wide', 'blk')), may hold values from -6 to 6
- right_points: float32 [2048], P('blk'), may hold values from -1 to 1
- right_ports: int32 [2048], P('blk'), may hold values from 0 to 63
- right_values: bfloat16 [2048, 64], P('blk'), may hold values from -6 to 6
- sketch_block: int32 [2048], P('blk'), may hold values from 0 to 63, as said below
- sketch_weight: bfloat16 [2048], P('blk'), may hold values from -1 to 1
Outputs:
- basis: float32 [4096, 64], P(('wide', 'blk'))
- projected: float32 [64, 64], replicated
Inputs may be any that keep to these rules, and one draw needn't show every extreme that they name: `left_points`: no left point lies closer than 0.6 / 2048 to any right point. `sketch_block`: in every aligned run of 64 right samples each sketch column appears exactly once.
All inputs are finite; a program needn't handle non-finite values.
Results may differ from a plain program's by a relative error of at most 0.0019.
Values sent between devices are 32-bit elements; how exact they have to be, the bound alone decides.
No kernel may reach another device: no remote copies, remote signals or barrier semaphores. Data moves between devices by JAX's collectives and lax.ppermute only.
A program may use at most 64 MiB of HBM per device.

v0:
```python
import jax
import jax.numpy as jnp
from jax import lax
from jax.sharding import PartitionSpec as P

K = 64


def cholesky_lower(gram):
    order = gram.shape[0]
    index_ids = jnp.arange(order, dtype=jnp.int32)

    def column_step(j, lower):
        row_j = lax.dynamic_slice_in_dim(lower, j, 1, 0)[0]
        column = lax.dynamic_slice_in_dim(gram, j, 1, 1)[:, 0] - jnp.dot(
            lower, row_j, precision=lax.Precision.HIGHEST
        )
        pivot = jnp.sqrt(lax.dynamic_slice_in_dim(column, j, 1, 0)[0])
        fresh = jnp.where(
            index_ids > j,
            column / pivot,
            jnp.where(index_ids == j, pivot, jnp.zeros((), gram.dtype)),
        )
        marker = (index_ids == j).astype(gram.dtype)
        return lower + fresh[:, None] * marker[None, :]

    return lax.fori_loop(0, order, column_step, jnp.zeros_like(gram))


def solve_lower(lower, rhs):
    order = lower.shape[0]
    index_ids = jnp.arange(order, dtype=jnp.int32)

    def row_step(j, result):
        row_j = lax.dynamic_slice_in_dim(lower, j, 1, 0)[0]
        pivot = lax.dynamic_slice_in_dim(row_j, j, 1, 0)[0]
        target = lax.dynamic_slice_in_dim(rhs, j, 1, 0)[0]
        value = (target - jnp.dot(row_j, result, precision=lax.Precision.HIGHEST)) / pivot
        marker = (index_ids == j).astype(rhs.dtype)
        return result + marker[:, None] * value[None, :]

    return lax.fori_loop(0, order, row_step, jnp.zeros_like(rhs))


def solve_upper(upper, rhs):
    order = upper.shape[0]
    index_ids = jnp.arange(order, dtype=jnp.int32)

    def row_step(step, result):
        j = order - 1 - step
        row_j = lax.dynamic_slice_in_dim(upper, j, 1, 0)[0]
        pivot = lax.dynamic_slice_in_dim(row_j, j, 1, 0)[0]
        target = lax.dynamic_slice_in_dim(rhs, j, 1, 0)[0]
        value = (target - jnp.dot(row_j, result, precision=lax.Precision.HIGHEST)) / pivot
        marker = (index_ids == j).astype(rhs.dtype)
        return result + marker[:, None] * value[None, :]

    return lax.fori_loop(0, order, row_step, jnp.zeros_like(rhs))


def tile_sketch(left_freq, left_onehot, left_values, points, ports, values_block, columns, weights):
    amount = points.shape[0]
    block_count = amount // amount
    port_ids = jnp.arange(left_values.shape[1], dtype=jnp.int32)
    column_ids = jnp.arange(K, dtype=jnp.int32)

    def absorb(carry, items):
        freq, port_block, value_rows, column_block, weight_block = items
        onehot_right = (port_ids[:, None] == port_block[None, :]).astype(jnp.float32)
        num_v = jnp.dot(
            left_values,
            onehot_right,
            precision=lax.Precision.HIGHEST,
            preferred_element_type=jnp.float32,
        )
        num_w = lax.dot_general(
            left_onehot,
            value_rows,
            (((1,), (1,)), ((), ())),
            precision=lax.Precision.HIGHEST,
            preferred_element_type=jnp.float32,
        )
        inverse = 1.0 / (left_freq[:, None] - freq[None, :])
        loewner = (num_v - num_w) * inverse
        shifted = (left_freq[:, None] * num_v - freq[None, :] * num_w) * inverse
        omega = jnp.where(
            column_block[:, None] == column_ids[None, :],
            weight_block[:, None],
            jnp.zeros((), jnp.float32),
        )
        sketch_part = jnp.dot(
            loewner, omega, precision=lax.Precision.HIGHEST, preferred_element_type=jnp.float32
        )
        shift_part = jnp.dot(
            shifted, omega, precision=lax.Precision.HIGHEST, preferred_element_type=jnp.float32
        )
        return ((carry[0] + sketch_part, carry[1] + shift_part), None)

    row_count = left_values.shape[0]
    start_carry = (jnp.zeros((row_count, K), jnp.float32), jnp.zeros((row_count, K), jnp.float32))
    items = (
        points.reshape(block_count, amount),
        ports.reshape(block_count, amount),
        values_block.reshape(block_count, amount, values_block.shape[1]),
        columns.reshape(block_count, amount),
        weights.reshape(block_count, amount),
    )
    result, _ = lax.scan(absorb, start_carry, items)
    return result


def left_setup(points, ports, width):
    port_ids = jnp.arange(width, dtype=jnp.int32)
    onehot_left = (ports[:, None] == port_ids[None, :]).astype(jnp.float32)
    return (points, onehot_left)


def per_device(
    left_points,
    left_ports,
    left_values,
    right_points,
    right_ports,
    right_values,
    sketch_block,
    sketch_weight,
):
    row_count = left_points.shape[0]
    width = left_values.shape[1]
    left_wide = left_values.astype(jnp.float32)
    group_points, group_ports, group_values = (
        lax.all_gather(left_points, "blk", axis=0, tiled=True),
        lax.all_gather(left_ports, "blk", axis=0, tiled=True),
        lax.all_gather(left_wide, "blk", axis=0, tiled=True),
    )
    right_wide = right_values.astype(jnp.float32)
    weight_wide = sketch_weight.astype(jnp.float32)
    left_freq, left_onehot = left_setup(group_points, group_ports, width)
    sketch_part, shift_part = tile_sketch(
        left_freq,
        left_onehot,
        group_values,
        right_points,
        right_ports,
        right_wide,
        sketch_block,
        weight_wide,
    )
    stacked = lax.psum_scatter(
        jnp.concatenate([sketch_part, shift_part], axis=1), "blk", scatter_dimension=0, tiled=True
    )
    sketch = stacked[:, :K]
    shifted_sketch = stacked[:, K:]
    row_total = row_count * lax.axis_size("wide") * lax.axis_size("blk")
    gram_local = jnp.dot(sketch.T, sketch, precision=lax.Precision.HIGHEST)
    gram = lax.psum(gram_local, ("wide", "blk")) / row_total
    lower = cholesky_lower(gram)
    basis_t = solve_lower(lower, sketch.T)
    projection_local = jnp.dot(basis_t, shifted_sketch, precision=lax.Precision.HIGHEST)
    coefficient = lax.psum(projection_local, ("wide", "blk")) / row_total
    projected = solve_upper(lower.T, coefficient)
    return (basis_t.T, projected)


def solution(mesh):
    placed = (
        P(("wide", "blk")),
        P(("wide", "blk")),
        P(("wide", "blk"), None),
        P("blk"),
        P("blk"),
        P("blk", None),
        P("blk"),
        P("blk"),
    )
    return jax.shard_map(
        per_device,
        mesh=mesh,
        in_specs=placed,
        out_specs=(P(("wide", "blk"), None), P()),
        check_vma=False,
    )
```

profile of v0, /device:TPU:0, one launch (start us, length us, event | category | flops | bytes accessed | tf_op | source)
XLA Modules:
  0.0 438.6 jit_solution(5190188491721261414)
XLA Ops:
  7.9 15.1 %all_gather.9 = f32[512,64]{0,1:T(8,128)S(1)} all-gather(f32[128,64]{0,1:T(8,128)S(1)} %convert_element_type.55), channel_id=1, replica_groups=mesh['wide'=8,'blk'=4] {'blk'}, dimensions={0}, use_global_device_ids=true | all-gather | bytes 163840 | tf_op jit(solution)/shard_map/all_gather | solution.py:134
  23.7 11.2 %all-gather = s32[4,1,128]{2,1,0:T(1,128)S(1)} all-gather(s32[1,1,128]{2,1,0:T(1,128)S(1)} %bitcast.82), channel_id=1, replica_groups=mesh['wide'=8,'blk'=4] {'blk'}, dimensions={0}, use_global_device_ids=true | all-gather | bytes 2560 | tf_op jit(solution)/shard_map/all_gather | solution.py:133
  35.6 7.7 %all-gather.1 = f32[4,1,128]{2,1,0:T(1,128)S(1)} all-gather(f32[1,1,128]{2,1,0:T(1,128)S(1)} %bitcast.83), channel_id=1, replica_groups=mesh['wide'=8,'blk'=4] {'blk'}, dimensions={0}, use_global_device_ids=true | all-gather | bytes 2560 | tf_op jit(solution)/shard_map/all_gather | solution.py:132
  45.3 1.1 fusion.28
  46.4 1.0 fusion.33
  48.1 19.8 %reduce-scatter.2.cloned.1.call-done = f32[128,128]{0,1:T(8,128)} async-done(((f32[512,128]{0,1:T(8,128)}), f32[128,128]{0,1:T(8,128)}) %reduce-scatter.2.cloned.1.call-update) | async-done | bytes 65552 | tf_op jit(solution)/shard_map/reduce_scatter | solution.py:149
  67.9 1.0 fusion.55
  68.9 38.6 %psum.14 = f32[64,64]{1,0:T(8,128)S(1)} all-reduce(f32[64,64]{1,0:T(8,128)S(1)} %fusion.55), channel_id=1, replica_groups=mesh['wide'=8,'blk'=4] {'wide','blk'}, use_global_device_ids=true, to_apply=%region_1.2 | all-reduce | flops 4096 | bytes 32768 | tf_op jit(solution)/shard_map/psum | solution.py:156
  107.7 94.5 %while.57 = (s32[]{:T(128)}, f32[64,64]{1,0:T(8,128)S(1)}, f32[64,64]{0,1:T(8,128)S(1)}, s32[]{:T(128)}, s32[]{:T(128)}) while((s32[]{:T(128)}, f32[64,64]{1,0:T(8,128)S(1)}, f32[64,64]{0,1:T(8,128)S(1)}, s32[]{:T(128)}, s32[]{:T(128)}) %tuple.124), condition=%wide.region_3.4_spmd.clone.clone, body=%wide.region_2.3_spmd.clone.clone.sunk | while | flops 66051 | bytes 101992 | solution.py:27
  202.2 93.7 %while.55 = (s32[]{:T(128)}, f32[64,128]{1,0:T(8,128)S(1)}, f32[64,128]{1,0:T(8,128)S(1)}, f32[64,64]{1,0:T(8,128)S(1)}, s32[]{:T(128)}, /*index=5*/s32[]{:T(128)}, s32[]{:T(128)}) while((s32[]{:T(128)}, f32[64,128]{1,0:T(8,128)S(1)}, f32[64,128]{1,0:T(8,128)S(1)}, f32[64,64]{1,0:T(8,128)S(1)}, s32[]{:T(128)}, ...), condition=%wide.region_5.6_spmd.clone, body=%wide.region_4.5_spmd.clone.sunk | while | flops 131460 | bytes 102520 | solution.py:42
  202.8 0.8 fusion.76
  204.3 0.8 fusion.76
  205.7 0.8 fusion.76
  207.2 0.8 fusion.76
  208.7 0.8 fusion.76
  210.1 0.8 fusion.76
  211.6 0.8 fusion.76
  213.1 0.8 fusion.76
  214.5 0.8 fusion.76
  216.0 0.8 fusion.76
  217.5 0.8 fusion.76
  218.9 0.8 fusion.76
  220.4 0.8 fusion.76
  221.8 0.8 fusion.76
  223.3 0.8 fusion.76
  224.8 0.8 fusion.76
  226.2 0.8 fusion.76
  227.7 0.8 fusion.76
  229.2 0.8 fusion.76
  230.6 0.8 fusion.76
  232.1 0.8 fusion.76
  233.6 0.8 fusion.76
  235.0 0.8 fusion.76
  236.5 0.8 fusion.76
  238.0 0.8 fusion.76
  239.4 0.8 fusion.76
  240.9 0.8 fusion.76
  242.3 0.8 fusion.76
  243.8 0.8 fusion.76
  245.3 0.8 fusion.76
  246.7 0.8 fusion.76
  248.2 0.8 fusion.76
  249.7 0.8 fusion.76
  251.1 0.8 fusion.76
  254.1 0.8 fusion.76
  273.1 0.8 fusion.76
  276.0 0.8 fusion.76
  279.0 0.8 fusion.76
  281.9 0.8 fusion.76
  296.6 40.8 %psum.15 = f32[64,64]{1,0:T(8,128)S(1)} all-reduce(f32[64,64]{1,0:T(8,128)S(1)} %fusion.53), channel_id=1, replica_groups=mesh['wide'=8,'blk'=4] {'wide','blk'}, use_global_device_ids=true, to_apply=%region_6.7 | all-reduce | flops 4096 | bytes 32768 | tf_op jit(solution)/shard_map/psum | solution.py:160
  337.5 93.7 %while.56 = (s32[]{:T(128)}, f32[64,64]{1,0:T(8,128)S(1)}, f32[64,64]{1,0:T(8,128)S(1)}, f32[64,64]{1,0:T(8,128)S(1)}, s32[]{:T(128)}, /*index=5*/s32[]{:T(128)}, s32[]{:T(128)}, s32[]{:T(128)}) while((s32[]{:T(128)}, f32[64,64]{1,0:T(8,128)S(1)}, f32[64,64]{1,0:T(8,128)S(1)}, f32[64,64]{1,0:T(8,128)S(1)}, s32[]{:T(128)}, ...), condition=%wide.region_8.9_spmd.clone, body=%wide.region_7.8_spmd.clone.sunk | while | flops 65800 | bytes 69297 | solution.py:58
  342.5 0.8 fusion.79
  348.3 0.8 fusion.79
  355.6 0.8 fusion.79
  363.0 0.8 fusion.79
  370.3 0.8 fusion.79
  376.1 0.8 fusion.79
  383.5 0.8 fusion.79
  390.8 0.8 fusion.79
  398.1 0.8 fusion.79
  403.9 0.8 fusion.79
  411.3 0.8 fusion.79
  418.6 0.8 fusion.79
  425.9 0.8 fusion.79
  (880 shorter events, 207.0 us)
Async XLA Ops:
  7.2 37.4 %copy-start = (bf16[512,64]{0,1:T(8,128)(2,1)S(1)}, bf16[512,64]{0,1:T(8,128)(2,1)}, u32[]{:S(2)}) copy-start(bf16[512,64]{0,1:T(8,128)(2,1)} %param.19) | copy-start | bytes 196612
  7.2 60.7 %reduce-scatter.2.cloned.1.call-start = ((), (), s32[]{:S(2)}) async-start(), calls=%async_computation.1 | async-start | bytes 327680 | tf_op jit(solution)/shard_map/reduce_scatter | solution.py:149
  23.0 0.7 copy-start.6
  34.9 0.7 copy-start.7
  35.6 7.7 %copy-start.5 = (bf16[512]{0:T(512)(128)(2,1)S(1)}, bf16[512]{0:T(512)(128)(2,1)}, u32[]{:S(2)}) copy-start(bf16[512]{0:T(512)(128)(2,1)} %param.21) | copy-start | bytes 3076
  43.3 0.7 copy-start.4
  44.6 0.7 copy-start.8
  44.6 0.7 copy-start.9
  107.7 94.5 %copy-start.3 = (f32[128,128]{0,1:T(8,128)S(1)}, f32[128,128]{0,1:T(8,128)}, u32[]{:S(2)}) copy-start(f32[128,128]{0,1:T(8,128)} %reduce-scatter.2.cloned.1.call-done) | copy-start | bytes 196612
  295.9 0.6 copy-start.1
  431.2 0.6 copy-start.2
Sparse Core Ops, SparseCore 0:
  48.2 19.6 reduce-scatter.1
where the time goes:
time: 441 us; the launch traced here: 439 us
  local copies, waits for them, and re-layouts  119 us (27%)
  matrix products  114 us (26%)
  blocking collectives  113 us (26%)
  loops' own time  40.3 us (9%)
  waiting for transfers between devices  19.8 us (4%)
  other arithmetic  18.2 us (4%)
  between operations  14.2 us (3%)
    dot_general x128, matrix products, row_step(): jnp.dot(row_j, result, precision=lax.Precision.HIGHEST)  100 us
    dynamic_slice x128, local copies, waits for them, and re-layouts, row_step(): pivot = lax.dynamic_slice_in_dim(row_j, j, 1, 0)[0]  76.2 us
    psum x1, blocking collectives, per_device(): coefficient = lax.psum(projection_local, ('wide', 'blk')) / row_total  40.8 us
    another operation x1, loops' own time, cholesky_lower(): return lax.fori_loop(0, order, column_step, jnp.zeros_like(gram))  40 us
    dynamic_slice x64, local copies, waits for them, and re-layouts, column_step(): pivot = jnp.sqrt(lax.dynamic_slice_in_dim(column, j, 1, 0)[0])  39.2 us
    psum x1, blocking collectives, per_device(): gram = lax.psum(gram_local, ('wide', 'blk')) / row_total  38.6 us
    reduce_scatter x1, waiting for transfers between devices, per_device(): lax.psum_scatter(jnp.concatenate([sketch_part, shift_part], axis=1), 'blk...  19.8 us
    all_gather x1, blocking collectives, per_device(): lax.all_gather(left_wide, 'blk', axis=0, tiled=True)  15.1 us
  transfers between devices with their start and end apart: 1, of which 1 were waited for; matrix products, arithmetic and copies ran while one was open for 0% of the time, Pallas kernels for 0%

commit v1 on v0

--- a/solution.py
+++ b/solution.py
@@ -4,6 +4,12 @@
 from jax.sharding import PartitionSpec as P
 
 K = 64
+
+
+def summed_here(x, mesh_axis):
+    parts = lax.all_gather(x, mesh_axis, axis=0, tiled=False)
+    summed = parts.sum(axis=0)
+    return summed
 
 
 def cholesky_lower(gram):
@@ -157,7 +163,7 @@
     lower = cholesky_lower(gram)
     basis_t = solve_lower(lower, sketch.T)
     projection_local = jnp.dot(basis_t, shifted_sketch, precision=lax.Precision.HIGHEST)
-    coefficient = lax.psum(projection_local, ("wide", "blk")) / row_total
+    coefficient = summed_here(projection_local, ("wide", "blk")) / row_total
     projected = solve_upper(lower.T, coefficient)
     return (basis_t.T, projected)
 

time: 441 us -> 476 us (1.079)
  blocking collectives: 113 us -> 148 us
    all_gather x0 -> x1, blocking collectives: none -> 75.5 us  [summed_here(): parts = lax.all_gather(x, mesh_axis, axis=0, tiled=False)]
    psum x1 -> x0, blocking collectives: 40.8 us -> none  [per_device(): coefficient = lax.psum(projection_local, ('wide', 'blk')) / row_total]
where the time goes in v1:
time: 476 us; the launch traced here: 473 us
  blocking collectives  148 us (31%)
  local copies, waits for them, and re-layouts  119 us (25%)
  matrix products  114 us (24%)
  loops' own time  40.3 us (8%)
  waiting for transfers between devices  19.8 us (4%)
  other arithmetic  18.3 us (4%)
  between operations  14.2 us (3%)
    dot_general x128, matrix products, row_step(): jnp.dot(row_j, result, precision=lax.Precision.HIGHEST)  100 us
    dynamic_slice x128, local copies, waits for them, and re-layouts, row_step(): pivot = lax.dynamic_slice_in_dim(row_j, j, 1, 0)[0]  76.2 us
    all_gather x1, blocking collectives, summed_here(): parts = lax.all_gather(x, mesh_axis, axis=0, tiled=False)  75.5 us
    another operation x1, loops' own time, cholesky_lower(): return lax.fori_loop(0, order, column_step, jnp.zeros_like(gram))  40 us
    dynamic_slice x64, local copies, waits for them, and re-layouts, column_step(): pivot = jnp.sqrt(lax.dynamic_slice_in_dim(column, j, 1, 0)[0])  39.2 us
    psum x1, blocking collectives, per_device(): gram = lax.psum(gram_local, ('wide', 'blk')) / row_total  38.6 us
    reduce_scatter x1, waiting for transfers between devices, per_device(): lax.psum_scatter(jnp.concatenate([sketch_part, shift_part], axis=1), 'blk...  19.8 us
    all_gather x1, blocking collectives, per_device(): lax.all_gather(left_wide, 'blk', axis=0, tiled=True)  15.1 us
  transfers between devices with their start and end apart: 1, of which 1 were waited for; matrix products, arithmetic and copies ran while one was open for 0% of the time, Pallas kernels for 0%

profile of v1, /device:TPU:0, one launch (start us, length us, event | category | flops | bytes accessed | tf_op | source)
XLA Modules:
  0.0 473.4 jit_solution(7564404267348109461)
XLA Ops:
  7.9 15.1 %all_gather.15 = f32[512,64]{0,1:T(8,128)S(1)} all-gather(f32[128,64]{0,1:T(8,128)S(1)} %convert_element_type.55), channel_id=1, replica_groups=mesh['wide'=8,'blk'=4] {'blk'}, dimensions={0}, use_global_device_ids=true | all-gather | bytes 163840 | tf_op jit(solution)/shard_map/all_gather | solution.py:140
  23.7 11.2 %all-gather.1 = s32[4,1,128]{2,1,0:T(1,128)S(1)} all-gather(s32[1,1,128]{2,1,0:T(1,128)S(1)} %bitcast.84), channel_id=1, replica_groups=mesh['wide'=8,'blk'=4] {'blk'}, dimensions={0}, use_global_device_ids=true | all-gather | bytes 2560 | tf_op jit(solution)/shard_map/all_gather | solution.py:139
  35.6 7.7 %all-gather.2 = f32[4,1,128]{2,1,0:T(1,128)S(1)} all-gather(f32[1,1,128]{2,1,0:T(1,128)S(1)} %bitcast.85), channel_id=1, replica_groups=mesh['wide'=8,'blk'=4] {'blk'}, dimensions={0}, use_global_device_ids=true | all-gather | bytes 2560 | tf_op jit(solution)/shard_map/all_gather | solution.py:138
  45.3 1.1 fusion.28
  46.4 1.0 fusion.33
  48.2 19.8 %reduce-scatter.2.cloned.1.call-done = f32[128,128]{0,1:T(8,128)} async-done(((f32[512,128]{0,1:T(8,128)}), f32[128,128]{0,1:T(8,128)}) %reduce-scatter.2.cloned.1.call-update) | async-done | bytes 65552 | tf_op jit(solution)/shard_map/reduce_scatter | solution.py:155
  67.9 1.0 fusion.55
  68.9 38.6 %psum.7 = f32[64,64]{1,0:T(8,128)S(1)} all-reduce(f32[64,64]{1,0:T(8,128)S(1)} %fusion.55), channel_id=1, replica_groups=mesh['wide'=8,'blk'=4] {'wide','blk'}, use_global_device_ids=true, to_apply=%region_1.2 | all-reduce | flops 4096 | bytes 32768 | tf_op jit(solution)/shard_map/psum | solution.py:162
  107.7 94.5 %while.57 = (s32[]{:T(128)}, f32[64,64]{1,0:T(8,128)S(1)}, f32[64,64]{0,1:T(8,128)S(1)}, s32[]{:T(128)}, s32[]{:T(128)}) while((s32[]{:T(128)}, f32[64,64]{1,0:T(8,128)S(1)}, f32[64,64]{0,1:T(8,128)S(1)}, s32[]{:T(128)}, s32[]{:T(128)}) %tuple.124), condition=%wide.region_3.4_spmd.clone.clone, body=%wide.region_2.3_spmd.clone.clone.sunk | while | flops 66051 | bytes 101992 | solution.py:33
  202.2 93.7 %while.55 = (s32[]{:T(128)}, f32[64,128]{1,0:T(8,128)S(1)}, f32[64,128]{1,0:T(8,128)S(1)}, f32[64,64]{1,0:T(8,128)S(1)}, s32[]{:T(128)}, /*index=5*/s32[]{:T(128)}, s32[]{:T(128)}) while((s32[]{:T(128)}, f32[64,128]{1,0:T(8,128)S(1)}, f32[64,128]{1,0:T(8,128)S(1)}, f32[64,64]{1,0:T(8,128)S(1)}, s32[]{:T(128)}, ...), condition=%wide.region_5.6_spmd.clone, body=%wide.region_4.5_spmd.clone.sunk | while | flops 131460 | bytes 102520 | solution.py:48
  202.8 0.8 fusion.76
  204.3 0.8 fusion.76
  205.8 0.8 fusion.76
  207.2 0.8 fusion.76
  208.7 0.8 fusion.76
  210.1 0.8 fusion.76
  211.6 0.8 fusion.76
  213.1 0.8 fusion.76
  214.5 0.8 fusion.76
  216.0 0.8 fusion.76
  217.5 0.8 fusion.76
  218.9 0.8 fusion.76
  220.4 0.8 fusion.76
  221.9 0.8 fusion.76
  223.3 0.8 fusion.76
  224.8 0.8 fusion.76
  226.2 0.8 fusion.76
  227.7 0.8 fusion.76
  229.2 0.8 fusion.76
  230.6 0.8 fusion.76
  232.1 0.8 fusion.76
  233.6 0.8 fusion.76
  235.0 0.8 fusion.76
  236.5 0.8 fusion.76
  238.0 0.8 fusion.76
  239.4 0.8 fusion.76
  240.9 0.8 fusion.76
  242.4 0.8 fusion.76
  243.8 0.8 fusion.76
  245.3 0.8 fusion.76
  246.7 0.8 fusion.76
  248.2 0.8 fusion.76
  249.7 0.8 fusion.76
  251.1 0.8 fusion.76
  252.6 0.8 fusion.76
  270.2 0.8 fusion.76
  273.1 0.8 fusion.76
  276.0 0.8 fusion.76
  279.0 0.8 fusion.76
  296.6 75.5 %all-gather = f32[2048,64]{1,0:T(8,128)S(1)} all-gather(f32[64,64]{1,0:T(8,128)S(1)} %fusion.53), channel_id=2, replica_groups=mesh['wide'=8,'blk'=4] {'wide','blk'}, dimensions={0}, use_global_device_ids=true | all-gather | bytes 540672 | tf_op jit(solution)/shard_map/all_gather | solution.py:10
  372.3 93.7 %while.56 = (s32[]{:T(128)}, f32[64,64]{1,0:T(8,128)S(1)}, f32[64,64]{1,0:T(8,128)S(1)}, f32[64,64]{1,0:T(8,128)S(1)}, s32[]{:T(128)}, /*index=5*/s32[]{:T(128)}, s32[]{:T(128)}, s32[]{:T(128)}) while((s32[]{:T(128)}, f32[64,64]{1,0:T(8,128)S(1)}, f32[64,64]{1,0:T(8,128)S(1)}, f32[64,64]{1,0:T(8,128)S(1)}, s32[]{:T(128)}, ...), condition=%wide.region_8.9_spmd.clone, body=%wide.region_7.8_spmd.clone.sunk | while | flops 65800 | bytes 69297 | solution.py:64
  375.8 0.8 fusion.79
  383.1 0.8 fusion.79
  389.0 0.8 fusion.79
  396.3 0.8 fusion.79
  403.6 0.8 fusion.79
  410.9 0.8 fusion.79
  416.8 0.8 fusion.79
  424.1 0.8 fusion.79
  431.4 0.8 fusion.79
  438.7 0.8 fusion.79
  444.6 0.8 fusion.79
  451.9 0.8 fusion.79
  459.2 0.8 fusion.79
  (881 shorter events, 207.1 us)
Async XLA Ops:
  7.2 37.4 %copy-start = (bf16[512,64]{0,1:T(8,128)(2,1)S(1)}, bf16[512,64]{0,1:T(8,128)(2,1)}, u32[]{:S(2)}) copy-start(bf16[512,64]{0,1:T(8,128)(2,1)} %param.19) | copy-start | bytes 196612
  7.2 60.7 %reduce-scatter.2.cloned.1.call-start = ((), (), s32[]{:S(2)}) async-start(), calls=%async_computation.1 | async-start | bytes 327680 | tf_op jit(solution)/shard_map/reduce_scatter | solution.py:155
  23.0 0.7 copy-start.6
  34.9 0.7 copy-start.7
  35.6 7.7 %copy-start.5 = (bf16[512]{0:T(512)(128)(2,1)S(1)}, bf16[512]{0:T(512)(128)(2,1)}, u32[]{:S(2)}) copy-start(bf16[512]{0:T(512)(128)(2,1)} %param.21) | copy-start | bytes 3076
  43.3 0.7 copy-start.4
  44.6 0.7 copy-start.8
  44.6 0.7 copy-start.9
  107.7 94.5 %copy-start.3 = (f32[128,128]{0,1:T(8,128)S(1)}, f32[128,128]{0,1:T(8,128)}, u32[]{:S(2)}) copy-start(f32[128,128]{0,1:T(8,128)} %reduce-scatter.2.cloned.1.call-done) | copy-start | bytes 196612
  295.9 0.6 copy-start.1
  466.0 0.6 copy-start.2
Sparse Core Ops, SparseCore 0:
  48.2 19.6 reduce-scatter.1
